TPU v7x, 128 devices: a whole 4x4x4 slice. The times are simulated.
128 devices in a mesh: seq: 4 (over z), exp: 32 (over y, x, core).
Axes of the slice: x: 4, y: 4, z: 4, core: 2. Of those that a mesh axis runs over, the one named last changes fastest.
Arguments:
- attn_inputs: bfloat16 [32, 512, 6144], P('exp', 'seq'), may hold values from -8 to 8
- residual: bfloat16 [32, 512, 2048], P('exp', 'seq'), may hold values from -6 to 6
- out_weight: bfloat16 [2048, 2048], P('exp'), may hold values from -0.125 to 0.125
- norm_gain: float32 [2048], replicated, may hold values from 0.1 to 1.9
- expert_ids: int32 [32, 512, 2], P('exp', 'seq'), may hold values from 0 to 31, all different within a row; in each aligned block of 128 rows (0 to 127, 128 to 255, ..., all dimensions but the last counted through in order) at most 10 rows name the same one
- gate_weights: float32 [32, 512, 2], P('exp', 'seq'), may hold values from 0.1 to 1
- gate_weight: bfloat16 [32, 2048, 5632], P('exp', None, 'seq'), may hold values from -0.125 to 0.125
- up_weight: bfloat16 [32, 2048, 5632], P('exp', None, 'seq'), may hold values from -0.125 to 0.125
- down_weight: bfloat16 [32, 5632, 2048], P('exp', 'seq'), may hold values from -0.078125 to 0.078125
Outputs:
- layer_out: bfloat16 [32, 512, 2048], P('exp', 'seq')
Inputs may be any that keep to these rules, and one draw needn't show every extreme that they name: `expert_ids`: each token names 2 different experts; in every draw no expert is named by more than 10 of the 128 tokens of one aligned block of rows (the rows of one device), and some block reaches 10.
All inputs are finite; a program needn't handle non-finite values.
Results may differ from a plain program's by a relative error of at most 0.013.
Values may be sent and summed in bfloat16 or wider, within the bound.
A program may use at most 128 MiB of HBM per device.

v0:
```python
import jax
import jax.numpy as jnp
from jax import lax
from jax.sharding import PartitionSpec as P

HEADS = 16
HEAD_DIM = 128
TOP = 2


def attend_block(query_block, key_rows, value_rows):
    scores = jnp.einsum(
        "qhd,khd->hqk", query_block, key_rows, preferred_element_type=jnp.float32
    ) * HEAD_DIM ** (-0.5)
    attn_probs = jax.nn.softmax(scores, axis=-1).astype(jnp.bfloat16)
    mixed_heads = jnp.einsum(
        "hqk,khd->qhd", attn_probs, value_rows, preferred_element_type=jnp.float32
    )
    return mixed_heads.astype(jnp.bfloat16)


def expert_rows_apply(tok_rows, gate_mat, up_mat, down_mat):
    gate_val = jnp.dot(tok_rows, gate_mat, preferred_element_type=jnp.float32)
    up_val = jnp.dot(tok_rows, up_mat, preferred_element_type=jnp.float32)
    hidden = (jax.nn.silu(gate_val) * up_val).astype(jnp.bfloat16)
    return jnp.dot(hidden, down_mat, preferred_element_type=jnp.float32)


def per_device(
    attn_inputs,
    residual,
    out_weight,
    norm_gain,
    expert_ids,
    gate_weights,
    gate_weight,
    up_weight,
    down_weight,
):
    tok_count = attn_inputs.shape[1]
    seq_count = lax.axis_size("seq")
    expert_count = lax.axis_size("exp")
    model_width = residual.shape[-1]
    head_local = HEADS // seq_count
    laid = attn_inputs.reshape(tok_count, 3, seq_count, head_local * HEAD_DIM)
    by_heads = lax.all_to_all(laid, "seq", split_axis=2, concat_axis=0, tiled=True)
    clip_len = by_heads.shape[0]
    queries = by_heads[:, 0, 0].reshape(clip_len, head_local, HEAD_DIM)
    keys_all = by_heads[:, 1, 0].reshape(clip_len, head_local, HEAD_DIM)
    values_all = by_heads[:, 2, 0].reshape(clip_len, head_local, HEAD_DIM)
    block_rows = min(512, clip_len)
    query_blocks = queries.reshape(clip_len // block_rows, block_rows, head_local, HEAD_DIM)
    attended = lax.map(lambda block: attend_block(block, keys_all, values_all), query_blocks)
    attended = attended.reshape(clip_len, head_local * HEAD_DIM)
    merged = lax.all_to_all(attended, "seq", split_axis=0, concat_axis=1, tiled=True)
    projected = jnp.dot(
        merged,
        lax.all_gather(out_weight, "exp", axis=0, tiled=True),
        preferred_element_type=jnp.float32,
    )
    middle = lax.optimization_barrier(
        (residual.reshape(tok_count, model_width).astype(jnp.float32) + projected).astype(
            jnp.bfloat16
        )
    )
    mid_float = middle.astype(jnp.float32)
    normed = (
        mid_float
        * lax.rsqrt(jnp.mean(mid_float * mid_float, axis=-1, keepdims=True) + 1e-06)
        * norm_gain
    ).astype(jnp.bfloat16)
    capacity = 5 * tok_count // (2 * expert_count)
    route_ids = expert_ids.reshape(tok_count * TOP)
    one_hot = (route_ids[:, None] == jnp.arange(expert_count, dtype=jnp.int32)[None, :]).astype(
        jnp.int32
    )
    before = jnp.cumsum(one_hot, axis=0) - one_hot
    slot_ids = jnp.sum(before * one_hot, axis=-1)
    target = route_ids * capacity + slot_ids
    placing = (
        target[None, :] == jnp.arange(expert_count * capacity, dtype=jnp.int32)[:, None]
    ).astype(jnp.bfloat16)
    pair_rows = jnp.repeat(normed, TOP, axis=0)
    slotted = jnp.dot(placing, pair_rows, preferred_element_type=jnp.float32).astype(jnp.bfloat16)
    gate_mat = gate_weight[0]
    up_mat = up_weight[0]
    down_mat = down_weight[0]
    copies = jnp.broadcast_to(slotted[None], (seq_count, expert_count * capacity, model_width))
    copies = copies.reshape(seq_count * expert_count, capacity, model_width)
    arrived = lax.all_to_all(copies, ("seq", "exp"), split_axis=0, concat_axis=0, tiled=True)
    partial_value = expert_rows_apply(
        arrived.reshape(-1, model_width), gate_mat, up_mat, down_mat
    ).astype(jnp.bfloat16)
    partial_value = partial_value.reshape(seq_count * expert_count, capacity, model_width)
    returned = lax.all_to_all(
        partial_value, ("seq", "exp"), split_axis=0, concat_axis=0, tiled=True
    )
    returned = returned.reshape(seq_count, expert_count * capacity, model_width)
    expert_out = jnp.sum(returned.astype(jnp.float32), axis=0).astype(jnp.bfloat16)
    picked = jnp.dot(placing.T, expert_out, preferred_element_type=jnp.float32)
    weighted = picked.reshape(tok_count, TOP, model_width) * gate_weights.reshape(tok_count, TOP, 1)
    result = mid_float + jnp.sum(weighted, axis=1)
    return result.astype(jnp.bfloat16).reshape(1, tok_count, model_width)


def solution(mesh):
    placed = (
        P("exp", "seq", None),
        P("exp", "seq", None),
        P("exp", None),
        P(),
        P("exp", "seq", None),
        P("exp", "seq", None),
        P("exp", None, "seq"),
        P("exp", None, "seq"),
        P("exp", "seq", None),
    )
    return jax.shard_map(
        per_device, mesh=mesh, in_specs=placed, out_specs=P("exp", "seq", None), check_vma=False
    )
```

profile of v0, /device:TPU:1, one launch (start us, length us, event | category | flops | bytes accessed | tf_op | source)
XLA Modules:
  0.0 375.0 jit_solution(14573751972843532361)
XLA Ops:
  6.5 0.0 all-gather.2.cloned.1.call-start
  6.5 0.7 all-gather.2.cloned.1.call-update
  7.3 1.9 copy.41
  9.2 1.3 copy.42
  10.5 5.9 %all-to-all-start = ((bf16[128,3,4,512]{0,3,1,2:T(8,128)(2,1)}), bf16[128,3,4,512]{0,3,1,2:T(8,128)(2,1)S(1)}, u32[]{:S(2)}, u32[]{:S(2)}) async-start(bf16[128,3,4,512]{0,3,1,2:T(8,128)(2,1)} %copy.42), calls=%async_computation | async-start | bytes 3145728 | tf_op jit(solution)/shard_map/all_to_all | solution.py:46
  16.4 0.0 copy-done.2
  16.4 0.1 copy.53
  16.5 0.1 eq.47
  16.6 0.6 reduce-window.6
  17.2 18.9 %all-to-all-done = bf16[128,3,4,512]{0,3,1,2:T(8,128)(2,1)S(1)} async-done(((bf16[128,3,4,512]{0,3,1,2:T(8,128)(2,1)}), bf16[128,3,4,512]{0,3,1,2:T(8,128)(2,1)S(1)}, u32[]{:S(2)}, u32[]{:S(2)}) %all-to-all-start) | async-done | bytes 1572896 | tf_op jit(solution)/shard_map/all_to_all | solution.py:46
  36.2 0.7 copy.43
  36.9 0.1 fusion.33
  37.0 0.2 copy.45
  37.2 0.2 copy.48
  37.4 0.2 copy.44
  37.6 3.5 fusion.34
  41.1 3.1 fusion.17
  44.3 0.4 copy.51
  44.7 1.0 all_to_all.37
  45.7 3.5 all-to-all-start.1
  49.2 0.2 slice_reduce_fusion
  49.3 0.1 reshape.85
  49.5 0.1 fusion.29
  49.6 6.5 %all-to-all-done.1 = bf16[4,128,512]{2,1,0:T(8,128)(2,1)S(1)} async-done(((bf16[4,128,512]{2,1,0:T(8,128)(2,1)}), bf16[4,128,512]{2,1,0:T(8,128)(2,1)S(1)}, u32[]{:S(2)}, u32[]{:S(2)}) %all-to-all-start.1) | async-done | bytes 524320 | tf_op jit(solution)/shard_map/all_to_all | solution.py:55
  56.1 0.3 copy.52
  56.4 9.7 %all-gather.2.cloned.1.call-done = bf16[2048,2048]{1,0:T(8,128)(2,1)} async-done(((bf16[64,2048]{1,0:T(8,128)(2,1)}), bf16[2048,2048]{1,0:T(8,128)(2,1)}) %all-gather.2.cloned.1.call-update) | async-done | bytes 8388624 | tf_op jit(solution)/shard_map/all_gather | solution.py:58
  66.1 0.0 copy-done
  66.1 4.7 %fusion.11 = bf16[128,2048]{1,0:T(8,128)(2,1)S(1)} fusion(bf16[128,2048]{0,1:T(8,128)(2,1)S(1)} %bitcast.66, bf16[2048,2048]{1,0:T(8,128)(2,1)} %all-gather.2.cloned.1.call-done, bf16[1,128,2048]{2,1,0:T(8,128)(2,1)S(1)} %copy-done), kind=kOutput, calls=%fused_computation.15 | convolution fusion | flops 1074528256 | bytes 9961472 | tf_op jit(solution)/shard_map/dot_general | solution.py:56
  70.7 0.2 fusion.18
  70.9 0.2 fusion.20
  71.1 0.6 broadcast_in_dim.11
  71.8 0.4 reshape.87
  72.2 0.5 convolution_convert_fusion.1
  72.7 3.0 broadcast_in_dim.12
  75.8 9.5 %reshape.88 = bf16[128,10,2048]{2,1,0:T(8,128)(2,1)} reshape(bf16[4,320,2048]{2,1,0:T(8,128)(2,1)} %broadcast_in_dim.12) | data formatting | bytes 10485760 | tf_op jit(solution)/shard_map/reshape | solution.py:89
  85.3 105.5 %all_to_all.47 = bf16[128,10,2048]{2,1,0:T(8,128)(2,1)} all-to-all(bf16[128,10,2048]{2,1,0:T(8,128)(2,1)} %reshape.88), channel_id=1, replica_groups=mesh['seq'=4,'exp'=32] {'seq','exp'}, dimensions={0} | all-to-all | bytes 10485760 | tf_op jit(solution)/shard_map/all_to_all | solution.py:90
  190.9 9.8 %reshape.89 = bf16[1280,2048]{1,0:T(8,128)(2,1)} reshape(bf16[128,10,2048]{2,1,0:T(8,128)(2,1)} %all_to_all.47) | data formatting | bytes 10485760 | tf_op jit(solution)/shard_map/reshape | solution.py:92
  200.7 13.6 %fusion.4 = f32[1280,1408]{1,0:T(8,128)} fusion(bf16[1280,2048]{1,0:T(8,128)(2,1)} %reshape.89, bf16[1,2048,1408]{2,1,0:T(8,128)(2,1)} %param.15), kind=kOutput, calls=%fused_computation.6 | convolution fusion | flops 7381975040 | bytes 18219008 | tf_op jit(solution)/shard_map/dot_general | solution.py:23
  214.3 24.7 %convolution_convert_fusion = bf16[1280,2048]{1,0:T(8,128)(2,1)} fusion(bf16[1,1408,2048]{2,1,0:T(8,128)(2,1)} %param.17, bf16[1280,2048]{1,0:T(8,128)(2,1)} %reshape.89, f32[1280,1408]{1,0:T(8,128)} %fusion.4, bf16[1,2048,1408]{2,1,0:T(8,128)(2,1)} %param.16), kind=kOutput, calls=%fused_computation.3 | convolution fusion | flops 14777384960 | bytes 29229056 | tf_op jit(solution)/shard_map/dot_general | solution.py:26
  239.0 9.5 %reshape.90 = bf16[128,10,2048]{2,1,0:T(8,128)(2,1)} reshape(bf16[1280,2048]{1,0:T(8,128)(2,1)} %convolution_convert_fusion) | data formatting | bytes 10485760 | tf_op jit(solution)/shard_map/reshape | solution.py:94
  248.6 5.6 %all-to-all-start.3 = ((bf16[128,10,2048]{2,1,0:T(8,128)(2,1)}), bf16[128,10,2048]{2,1,0:T(8,128)(2,1)}, u32[]{:S(2)}, u32[]{:S(2)}) async-start(bf16[128,10,2048]{2,1,0:T(8,128)(2,1)} %reshape.90), calls=%async_computation.3 | async-start | bytes 16777216 | tf_op jit(solution)/shard_map/all_to_all | solution.py:95
  254.1 0.1 reduce_sum.53
  254.3 0.1 copy.57
  254.4 98.6 %all-to-all-done.3 = bf16[128,10,2048]{2,1,0:T(8,128)(2,1)} async-done(((bf16[128,10,2048]{2,1,0:T(8,128)(2,1)}), bf16[128,10,2048]{2,1,0:T(8,128)(2,1)}, u32[]{:S(2)}, u32[]{:S(2)}) %all-to-all-start.3) | async-done | bytes 5242912 | tf_op jit(solution)/shard_map/all_to_all | solution.py:95
  353.0 9.8 %reshape.91 = bf16[4,320,2048]{2,1,0:T(8,128)(2,1)} reshape(bf16[128,10,2048]{2,1,0:T(8,128)(2,1)} %all-to-all-done.3) | data formatting | bytes 10485760 | tf_op jit(solution)/shard_map/reshape | solution.py:98
  362.8 3.6 reduce_sum.55
  366.4 0.8 fusion.14
  367.2 0.9 fusion.22
  (12 shorter events, 0.1 us)
Async XLA Ops:
  6.5 9.8 %copy-start.2 = (s32[1,128,2]{1,2,0:T(2,128)S(1)}, s32[1,128,2]{1,2,0:T(2,128)}, u32[]{:S(2)}) copy-start(s32[1,128,2]{1,2,0:T(2,128)} %param.13) | copy-start | bytes 3076
  6.5 59.5 %all-gather.2.cloned.1.call-start = ((), (), s32[]{:S(2)}) async-start(), calls=%async_computation.4 | async-start | bytes 8650752 | tf_op jit(solution)/shard_map/all_gather | solution.py:58
  10.5 25.7 %all-to-all-start = ((bf16[128,3,4,512]{0,3,1,2:T(8,128)(2,1)}), bf16[128,3,4,512]{0,3,1,2:T(8,128)(2,1)S(1)}, u32[]{:S(2)}, u32[]{:S(2)}) async-start(bf16[128,3,4,512]{0,3,1,2:T(8,128)(2,1)} %copy.42), calls=%async_computation | async-start | bytes 3145728 | tf_op jit(solution)/shard_map/all_to_all | solution.py:46
  41.1 24.9 %copy-start = (bf16[1,128,2048]{2,1,0:T(8,128)(2,1)S(1)}, bf16[1,128,2048]{2,1,0:T(8,128)(2,1)}, u32[]{:S(2)}) copy-start(bf16[1,128,2048]{2,1,0:T(8,128)(2,1)} %param.10) | copy-start | bytes 1572868
  45.7 10.4 %all-to-all-start.1 = ((bf16[4,128,512]{2,1,0:T(8,128)(2,1)}), bf16[4,128,512]{2,1,0:T(8,128)(2,1)S(1)}, u32[]{:S(2)}, u32[]{:S(2)}) async-start(bf16[4,128,512]{2,1,0:T(8,128)(2,1)} %all_to_all.37), calls=%async_computation.1 | async-start | bytes 1048576 | tf_op jit(solution)/shard_map/all_to_all | solution.py:55
  66.1 4.9 %copy-start.1 = (f32[2048]{0:T(1024)S(1)}, f32[2048]{0:T(1024)}, u32[]{:S(2)}) copy-start(f32[2048]{0:T(1024)} %param.12) | copy-start | bytes 24580
  248.6 104.4 %all-to-all-start.3 = ((bf16[128,10,2048]{2,1,0:T(8,128)(2,1)}), bf16[128,10,2048]{2,1,0:T(8,128)(2,1)}, u32[]{:S(2)}, u32[]{:S(2)}) async-start(bf16[128,10,2048]{2,1,0:T(8,128)(2,1)} %reshape.90), calls=%async_computation.3 | async-start | bytes 16777216 | tf_op jit(solution)/shard_map/all_to_all | solution.py:95
  362.8 3.6 copy-start.3
Sparse Core Ops, SparseCore 0:
  9.6 56.3 all-gather.1
where the time goes:
time: 380 us; the launch traced here: 375 us
  waiting for transfers between devices  134 us (35%)
  blocking collectives  106 us (28%)
  matrix products  50.9 us (13%)
  local copies, waits for them, and re-layouts  50 us (13%)
  starting transfers between devices  14.9 us (4%)
  between operations  13.6 us (4%)
  other arithmetic  5.67 us (1%)
    all_to_all x1, blocking collectives, per_device(): lax.all_to_all(copies, ('seq', 'exp'), split_axis=0, concat_axis=0, tiled...  106 us
    all_to_all x1, waiting for transfers between devices, per_device(): lax.all_to_all(partial_value, ('seq', 'exp'), split_axis=0, concat_axis=0...  98.6 us
    dot_general x1, matrix products, expert_rows_apply(): return jnp.dot(hidden, down_mat, preferred_element_type=jnp.float32)  24.7 us
    all_to_all x1, waiting for transfers between devices, per_device(): lax.all_to_all(laid, 'seq', split_axis=2, concat_axis=0, tiled=True)  18.9 us
    dot_general x1, matrix products, expert_rows_apply(): gate_val = jnp.dot(tok_rows, gate_mat, preferred_element_type=jnp.float32)  13.6 us
    reshape x1, local copies, waits for them, and re-layouts, per_device(): arrived.reshape(-1, model_width)  9.85 us
    reshape x1, local copies, waits for them, and re-layouts, per_device(): returned = returned.reshape(seq_count, expert_count * capacity, model_width)  9.84 us
    all_gather x1, waiting for transfers between devices, per_device(): lax.all_gather(out_weight, 'exp', axis=0, tiled=True)  9.67 us
  transfers between devices with their start and end apart: 4, of which 4 were waited for; matrix products, arithmetic and copies ran while one was open for 4% of the time, Pallas kernels for 0%

commit v1 on v0

v1 whole, which is shorter than its diff:
```python
import functools

import jax
import jax.numpy as jnp
from jax import lax
from jax.experimental import pallas as pl
from jax.experimental.pallas import tpu as pltpu
from jax.sharding import PartitionSpec as P

HEADS = 16
HEAD_DIM = 128
TOP = 2
TOK = 128
D = 2048
FFL = 1408
EXPERTS = 32
MESH = pl.DeviceIdType.MESH
BF = jnp.bfloat16
F32 = jnp.float32
MAIN = 8
GROUPS = 4
QUART = D // 4


def attend_block(query_block, key_rows, value_rows):
    scores = jnp.einsum(
        "qhd,khd->hqk", query_block, key_rows, preferred_element_type=jnp.float32
    ) * HEAD_DIM ** (-0.5)
    attn_probs = jax.nn.softmax(scores, axis=-1).astype(jnp.bfloat16)
    mixed_heads = jnp.einsum(
        "hqk,khd->qhd", attn_probs, value_rows, preferred_element_type=jnp.float32
    )
    return mixed_heads.astype(jnp.bfloat16)


def position():
    s = lax.axis_index("seq")
    e = lax.axis_index("exp")
    return s, lax.rem(lax.div(e, 8), 4), lax.rem(lax.div(e, 2), 4), lax.rem(e, 2)


def plane_device(s, y, x, c, i, sign):
    dy, dx, dc = lax.div(i, 8), lax.rem(lax.div(i, 2), 4), lax.rem(i, 2)
    ny = lax.rem(y + sign * dy + 4, 4)
    nx = lax.rem(x + sign * dx + 4, 4)
    nc = lax.rem(c + dc, 2)
    return (s, (ny * 4 + nx) * 2 + nc)


def rel_index(ids, y, x, c):
    dy = ((ids >> 3) + (4 - y)) & 3
    dx = (((ids >> 1) & 3) + (4 - x)) & 3
    dc = ((ids & 1) + c) & 1
    return dy * 8 + dx * 2 + dc


def onehot(cond):
    return jnp.where(cond, 1.0, 0.0)


def split_slot(rel, slot):
    main = jnp.where(slot < MAIN, rel * MAIN + slot, -1)
    tail = jnp.where(slot >= MAIN, rel * 2 + slot - MAIN, -1)
    return main, tail


def routes_cols(ids, y, x, c):
    lane = lax.broadcasted_iota(jnp.int32, (TOK, EXPERTS), 1)
    hot = [onehot(lane == ids[:, k : k + 1]) for k in range(TOP)]
    row = lax.broadcasted_iota(jnp.int32, (TOK, TOK), 0)
    col = lax.broadcasted_iota(jnp.int32, (TOK, TOK), 1)
    before = jnp.dot(
        onehot(col < row).astype(BF), (hot[0] + hot[1]).astype(BF), preferred_element_type=F32
    )
    out = []
    for k in range(TOP):
        slot = jnp.sum(hot[k] * before, axis=1, keepdims=True).astype(jnp.int32)
        out.append(split_slot(rel_index(ids[:, k : k + 1], y, x, c), slot))
    return out


def routes_rows(ids, y, x, c):
    sub = lax.broadcasted_iota(jnp.int32, (EXPERTS, TOK), 0)
    hot = [onehot(sub == ids[k : k + 1, :]) for k in range(TOP)]
    row = lax.broadcasted_iota(jnp.int32, (TOK, TOK), 0)
    col = lax.broadcasted_iota(jnp.int32, (TOK, TOK), 1)
    before = jnp.dot(
        (hot[0] + hot[1]).astype(BF), onehot(row < col).astype(BF), preferred_element_type=F32
    )
    out = []
    for k in range(TOP):
        slot = jnp.sum(hot[k] * before, axis=0, keepdims=True).astype(jnp.int32)
        out.append(split_slot(rel_index(ids[k : k + 1, :], y, x, c), slot))
    return out


def expert_kernel(
    normed,
    mid,
    ids,
    ids_t,
    gates,
    wg_hbm,
    wu_hbm,
    wd_hbm,
    out,
    wg,
    wu,
    wd,
    send_m,
    send_f,
    recv_m,
    recv_f,
    hid,
    part_m,
    part_f,
    far_m,
    far_f,
    sum_m,
    sum_f,
    near_m,
    near_f,
    red_m,
    red_f,
    back_m,
    back_f,
    w_sem,
    ip_s,
    ip_r,
    f_s,
    f_r,
    r_s,
    r_r,
    a_s,
    a_r,
    b_s,
    b_r,
    c_s,
    c_r,
    o_s,
    o_r,
):
    s, y, x, c = position()
    exp_me = (y * 4 + x) * 2 + c
    up = (lax.rem(s + 1, 4), exp_me)
    down = (lax.rem(s + 3, 4), exp_me)
    zdev = (up, down)

    def remote(src, dst, ss, rs, dev):
        return pltpu.make_async_remote_copy(
            src_ref=src, dst_ref=dst, send_sem=ss, recv_sem=rs, device_id=dev, device_id_type=MESH
        )

    barrier = pltpu.get_barrier_semaphore()

    @pl.loop(1, 32)
    def _(i):
        pl.semaphore_signal(
            barrier, inc=1, device_id=plane_device(s, y, x, c, i, 1), device_id_type=MESH
        )

    for dev in zdev:
        pl.semaphore_signal(barrier, inc=1, device_id=dev, device_id_type=MESH)

    loads = [
        pltpu.make_async_copy(h, v, w_sem.at[i])
        for i, (h, v) in enumerate(((wg_hbm, wg), (wu_hbm, wu), (wd_hbm, wd)))
    ]
    for ld in loads:
        ld.start()

    rows = routes_rows(ids_t[...], y, x, c)
    sub = lax.broadcasted_iota(jnp.int32, (EXPERTS * MAIN, TOK), 0)
    place = onehot((sub == rows[0][0]) | (sub == rows[1][0])).astype(BF)
    fold_place = [
        onehot((sub == rows[0][1] * 4 + k) | (sub == rows[1][1] * 4 + k)).astype(BF)
        for k in range(4)
    ]
    fold = None
    for k in range(4):
        cols = slice(k * QUART, (k + 1) * QUART)
        tokens = normed[:, cols]
        send_m[:, cols] = jnp.dot(place, tokens, preferred_element_type=F32).astype(BF)
        term = jnp.dot(fold_place[k], tokens, preferred_element_type=F32)
        fold = term if fold is None else fold + term
    send_f[...] = fold.astype(BF)
    recv_m[0, 0:MAIN, :] = send_m[0:MAIN, :]
    recv_f[0, 0:MAIN, :] = send_f[0:MAIN, :]

    pl.semaphore_wait(barrier, 33)

    def inplane(i):
        dev = plane_device(s, y, x, c, i, 1)
        g, k = lax.div(i, 8), lax.rem(i, 8)
        src = pl.ds(pl.multiple_of(i * MAIN, MAIN), MAIN)
        dst = pl.ds(pl.multiple_of(k * MAIN, MAIN), MAIN)
        return (
            remote(send_m.at[src], recv_m.at[g, dst], ip_s.at[i, 0], ip_r.at[i, 0], dev),
            remote(send_f.at[src], recv_f.at[g, dst], ip_s.at[i, 1], ip_r.at[i, 1], dev),
        )

    @pl.loop(1, 32)
    def _(i):
        for cp in inplane(i):
            cp.start()

    def ranges(size, off):
        return pl.ds(off, size)

    def pair(src_m, src_f, srow, dst_m, dst_f, drow, ss, rs, dev):
        return (
            remote(src_m.at[srow], dst_m.at[drow], ss.at[0], rs.at[0], dev),
            remote(src_f.at[srow], dst_f.at[drow], ss.at[1], rs.at[1], dev),
        )

    def forward(g, d):
        drow = ranges(64, 192 if d == 0 else 64)
        return pair(
            recv_m.at[g], recv_f.at[g], ranges(64, 0), recv_m.at[g], recv_f.at[g], drow,
            f_s.at[g, d], f_r.at[g, d], zdev[d],
        )

    def relay(g, d):
        srow = ranges(32, 192 if d == 0 else 96)
        drow = ranges(32, 128 if d == 0 else 160)
        return pair(
            recv_m.at[g], recv_f.at[g], srow, recv_m.at[g], recv_f.at[g], drow,
            r_s.at[g, d], r_r.at[g, d], zdev[d],
        )

    def far(g, d):
        srow = ranges(32, 128 if d == 0 else 160)
        return pair(
            part_m.at[g], part_f.at[g], srow, far_m.at[g, d], far_f.at[g, d], ranges(32, 0),
            a_s.at[g, d], a_r.at[g, d], zdev[d],
        )

    def direct(g, d):
        srow = ranges(32, 96 if d == 0 else 192)
        drow = ranges(32, 32 if d == 0 else 0)
        return pair(
            part_m.at[g], part_f.at[g], srow, near_m.at[g, d], near_f.at[g, d], drow,
            b_s.at[g, d], b_r.at[g, d], zdev[d],
        )

    def summed(g, d):
        drow = ranges(32, 0 if d == 0 else 32)
        return pair(
            sum_m.at[g, d], sum_f.at[g, d], ranges(32, 0), near_m.at[g, d], near_f.at[g, d], drow,
            c_s.at[g, d], c_r.at[g, d], zdev[d],
        )

    def home(g, k):
        i = g * 8 + k
        dev = plane_device(s, y, x, c, i, -1)
        src = pl.ds(pl.multiple_of(k * MAIN, MAIN), MAIN)
        dst = pl.ds(pl.multiple_of(i * MAIN, MAIN), MAIN)
        return (
            remote(red_m.at[g, src], back_m.at[dst], o_s.at[i, 0], o_r.at[i, 0], dev),
            remote(red_f.at[g, src], back_f.at[dst], o_s.at[i, 1], o_r.at[i, 1], dev),
        )

    def start(make, g):
        for d in range(2):
            for cp in make(g, d):
                cp.start()

    def arrived(make, g):
        for d in range(2):
            for cp in make(g, d):
                cp.wait_recv()

    def dispatch_group(g):
        @pl.loop(max(1, g * 8), g * 8 + 8)
        def _(i):
            for cp in inplane(i):
                cp.wait_recv()

        start(forward, g)

    def relay_group(g):
        arrived(forward, g)
        start(relay, g)

    perm_row = lax.broadcasted_iota(jnp.int32, (256, 256), 0)
    perm_col = lax.broadcasted_iota(jnp.int32, (256, 256), 1)

    def experts(g):
        arrived(relay, g)
        unfold = onehot(perm_col == (perm_row & 63) * 4 + (perm_row >> 6)).astype(BF)
        tail = jnp.dot(unfold, recv_f[g], preferred_element_type=F32).astype(BF)
        for k in range(4):
            recv_m[g, 256:320, k * QUART : (k + 1) * QUART] = tail[k * 64 : (k + 1) * 64, :]

        def hidden(cols):
            gate = jnp.dot(recv_m[g], wg[:, cols], preferred_element_type=F32)
            upv = jnp.dot(recv_m[g], wu[:, cols], preferred_element_type=F32)
            hid[:, cols] = (gate / (1.0 + jnp.exp(-gate)) * upv).astype(BF)

        @pl.loop(0, 5)
        def _(j):
            hidden(pl.ds(pl.multiple_of(j * 256, 256), 256))

        hidden(pl.ds(1280, 128))

        @pl.loop(0, 8)
        def _(j):
            cols = pl.ds(pl.multiple_of(j * 256, 256), 256)
            part_m[g, :, cols] = jnp.dot(
                hid[...], wd[:, cols], preferred_element_type=F32
            ).astype(BF)

        fold_back = onehot(perm_row == (perm_col & 63) * 4 + (perm_col >> 6)).astype(BF)
        stacked = jnp.concatenate(
            [part_m[g, 256:320, k * QUART : (k + 1) * QUART] for k in range(4)], axis=0
        )
        part_f[g] = jnp.dot(fold_back, stacked, preferred_element_type=F32).astype(BF)
        start(far, g)
        start(direct, g)

    def pass_sums(g):
        arrived(far, g)
        for d in range(2):
            own = pl.ds(64 if d == 0 else 224, 32)
            sum_m[g, d] = (part_m[g, own, :].astype(F32) + far_m[g, d].astype(F32)).astype(BF)
            sum_f[g, d] = (part_f[g, own, :].astype(F32) + far_f[g, d].astype(F32)).astype(BF)
        start(summed, g)

    def go_home(g):
        arrived(direct, g)
        arrived(summed, g)
        red_m[g] = (
            part_m[g, 0:64, :].astype(F32) + near_m[g, 0].astype(F32) + near_m[g, 1].astype(F32)
        ).astype(BF)
        red_f[g] = (
            part_f[g, 0:64, :].astype(F32) + near_f[g, 0].astype(F32) + near_f[g, 1].astype(F32)
        ).astype(BF)
        if g == 0:
            back_m[0:MAIN, :] = red_m[0, 0:MAIN, :]
            back_f[0:MAIN, :] = red_f[0, 0:MAIN, :]

        @pl.loop(1 if g == 0 else 0, 8)
        def _(k):
            for cp in home(g, k):
                cp.start()

    dispatch_group(0)
    dispatch_group(1)
    relay_group(0)
    dispatch_group(2)
    relay_group(1)
    dispatch_group(3)
    for ld in loads:
        ld.wait()
    experts(0)
    relay_group(2)
    experts(1)
    pass_sums(0)
    relay_group(3)
    experts(2)
    pass_sums(1)
    go_home(0)
    experts(3)
    pass_sums(2)
    go_home(1)
    pass_sums(3)
    go_home(2)
    go_home(3)

    cols_of = routes_cols(ids[...], y, x, c)
    lane = lax.broadcasted_iota(jnp.int32, (TOK, EXPERTS * MAIN), 1)

    @pl.loop(1, 32)
    def _(i):
        for cp in home(lax.div(i, 8), lax.rem(i, 8)):
            cp.wait_recv()

    for k in range(4):
        cols = slice(k * QUART, (k + 1) * QUART)
        total = mid[:, cols].astype(F32)
        for ch in range(TOP):
            main, tail = cols_of[ch]
            picked = jnp.dot(
                onehot(lane == main).astype(BF), back_m[:, cols], preferred_element_type=F32
            ) + jnp.dot(
                onehot(lane == tail * 4 + k).astype(BF), back_f[...], preferred_element_type=F32
            )
            total = total + picked * gates[:, ch : ch + 1]
        out[:, cols] = total.astype(BF)

    @pl.loop(1, 32)
    def _(i):
        for cp in inplane(i):
            cp.wait_send()
        for cp in home(lax.div(i, 8), lax.rem(i, 8)):
            cp.wait_send()

    for g in range(GROUPS):
        for make in (forward, relay, far, direct, summed):
            for d in range(2):
                for cp in make(g, d):
                    cp.wait_send()


def expert_stage(normed, middle, ids, gates, wg, wu, wd):
    vm = pl.BlockSpec(memory_space=pltpu.VMEM)
    hb = pl.BlockSpec(memory_space=pl.ANY)
    dma = pltpu.SemaphoreType.DMA
    G = GROUPS
    scratch = [
        pltpu.VMEM((D, FFL), BF),
        pltpu.VMEM((D, FFL), BF),
        pltpu.VMEM((FFL, D), BF),
        pltpu.VMEM((256, D), BF),
        pltpu.VMEM((256, QUART), BF),
        pltpu.VMEM((G, 320, D), BF),
        pltpu.VMEM((G, 256, QUART), BF),
        pltpu.VMEM((320, FFL), BF),
        pltpu.VMEM((G, 320, D), BF),
        pltpu.VMEM((G, 256, QUART), BF),
        pltpu.VMEM((G, 2, 32, D), BF),
        pltpu.VMEM((G, 2, 32, QUART), BF),
        pltpu.VMEM((G, 2, 32, D), BF),
        pltpu.VMEM((G, 2, 32, QUART), BF),
        pltpu.VMEM((G, 2, 64, D), BF),
        pltpu.VMEM((G, 2, 64, QUART), BF),
        pltpu.VMEM((G, 64, D), BF),
        pltpu.VMEM((G, 64, QUART), BF),
        pltpu.VMEM((256, D), BF),
        pltpu.VMEM((256, QUART), BF),
        dma((3,)),
        dma((32, 2)),
        dma((32, 2)),
    ]
    scratch += [dma((G, 2, 2)) for _ in range(10)]
    scratch += [dma((32, 2)), dma((32, 2))]
    return pl.pallas_call(
        expert_kernel,
        out_shape=jax.ShapeDtypeStruct((TOK, D), BF),
        in_specs=[vm] * 5 + [hb] * 3,
        out_specs=vm,
        scratch_shapes=scratch,
        name="expert_stage",
        compiler_params=pltpu.CompilerParams(
            collective_id=0, has_side_effects=True, vmem_limit_bytes=60 * 2**20
        ),
    )(normed, middle, ids, ids.T, gates, wg, wu, wd)


def per_device(
    attn_inputs,
    residual,
    out_weight,
    norm_gain,
    expert_ids,
    gate_weights,
    gate_weight,
    up_weight,
    down_weight,
):
    tok_count = attn_inputs.shape[1]
    seq_count = lax.axis_size("seq")
    model_width = residual.shape[-1]
    head_local = HEADS // seq_count
    laid = attn_inputs.reshape(tok_count, 3, seq_count, head_local * HEAD_DIM)
    by_heads = lax.all_to_all(laid, "seq", split_axis=2, concat_axis=0, tiled=True)
    clip_len = by_heads.shape[0]
    queries = by_heads[:, 0, 0].reshape(clip_len, head_local, HEAD_DIM)
    keys_all = by_heads[:, 1, 0].reshape(clip_len, head_local, HEAD_DIM)
    values_all = by_heads[:, 2, 0].reshape(clip_len, head_local, HEAD_DIM)
    attended = attend_block(queries, keys_all, values_all)
    attended = attended.reshape(clip_len, head_local * HEAD_DIM)
    merged = lax.all_to_all(attended, "seq", split_axis=0, concat_axis=1, tiled=True)
    projected = jnp.dot(
        merged,
        lax.all_gather(out_weight, "exp", axis=0, tiled=True),
        preferred_element_type=jnp.float32,
    )
    middle = lax.optimization_barrier(
        (residual.reshape(tok_count, model_width).astype(jnp.float32) + projected).astype(
            jnp.bfloat16
        )
    )
    mid_float = middle.astype(jnp.float32)
    normed = (
        mid_float
        * lax.rsqrt(jnp.mean(mid_float * mid_float, axis=-1, keepdims=True) + 1e-06)
        * norm_gain
    ).astype(jnp.bfloat16)
    result = expert_stage(
        normed,
        middle,
        expert_ids.reshape(tok_count, TOP),
        gate_weights.reshape(tok_count, TOP),
        gate_weight[0],
        up_weight[0],
        down_weight[0],
    )
    return result.reshape(1, tok_count, model_width)


def solution(mesh):
    placed = (
        P("exp", "seq", None),
        P("exp", "seq", None),
        P("exp", None),
        P(),
        P("exp", "seq", None),
        P("exp", "seq", None),
        P("exp", None, "seq"),
        P("exp", None, "seq"),
        P("exp", "seq", None),
    )
    return jax.shard_map(
        per_device, mesh=mesh, in_specs=placed, out_specs=P("exp", "seq", None), check_vma=False
    )
```

time: 380 us -> 200 us (0.53); the launches traced: 375 us -> 200 us
  Pallas kernels: 0 us -> 119 us
  waiting for transfers between devices: 134 us -> 17.1 us
  blocking collectives: 106 us -> 25.5 us
  local copies, waits for them, and re-layouts: 50 us -> 8.48 us
  matrix products: 50.9 us -> 11.2 us
  starting transfers between devices: 14.9 us -> 3.65 us
  other arithmetic: 5.67 us -> 1.18 us
    pallas_call x0 -> x1, Pallas kernels: none -> 119 us  [expert_stage(): pl.pallas_call(expert_kernel, out_shape=jax.ShapeDtypeStruct((TOK, D), BF...]
    all_to_all x2 -> x0, waiting for transfers between devices: 118 us -> none  [the longest x1 98.6 us: per_device(): lax.all_to_all(partial_value, ('seq', 'exp'), split_axis=0, concat_axis=0...]
    all_to_all x1, blocking collectives: 106 us -> 25.5 us  [per_device(): lax.all_to_all(laid, 'seq', split_axis=2, concat_axis=0, tiled=True)]
    dot_general x4 -> x0, matrix products: 39.6 us -> none  [the longest x1 24.7 us: expert_rows_apply(): return jnp.dot(hidden, down_mat, preferred_element_type=jnp.float32)]
    reshape x6 -> x1, local copies, waits for them, and re-layouts: 39.4 us -> 0.73 us  [per_device(): expert_ids.reshape(tok_count, TOP)]
    all_to_all x2 -> x0, starting transfers between devices: 11.4 us -> none  [the longest x1 5.86 us: per_device(): lax.all_to_all(laid, 'seq', split_axis=2, concat_axis=0, tiled=True)]
  transfers between devices with their start and end apart: 4 -> 2, of which waited for: 4 -> 2; matrix products, arithmetic and copies ran while one was open for 4% -> 6% of each run, Pallas kernels for 0% -> 0%
where the time goes in v1:
time: 200 us
  Pallas kernels  119 us (60%)
  blocking collectives  25.5 us (13%)
  waiting for transfers between devices  17.1 us (9%)
  between operations  13.5 us (7%)
  matrix products  11.2 us (6%)
  local copies, waits for them, and re-layouts  8.48 us (4%)
  starting transfers between devices  3.65 us (2%)
    pallas_call x1, Pallas kernels, expert_stage(): pl.pallas_call(expert_kernel, out_shape=jax.ShapeDtypeStruct((TOK, D), BF...  119 us
    all_to_all x1, blocking collectives, per_device(): lax.all_to_all(laid, 'seq', split_axis=2, concat_axis=0, tiled=True)  25.5 us
    all_gather x1, waiting for transfers between devices, per_device(): lax.all_gather(out_weight, 'exp', axis=0, tiled=True)  10.7 us
    all_to_all x1, waiting for transfers between devices, per_device(): lax.all_to_all(attended, 'seq', split_axis=0, concat_axis=1, tiled=True)  5.71 us
    dot_general x1, matrix products, per_device(): jnp.dot(merged, lax.all_gather(out_weight, 'exp', axis=0, tiled=True), pr...  4.67 us
    unnamed x13, local copies, waits for them, and re-layouts  4.54 us
  transfers between devices with their start and end apart: 2, of which 2 were waited for; matrix products, arithmetic and copies ran while one was open for 6% of the time, Pallas kernels for 0%

profile of v1, /device:TPU:1, one launch (start us, length us, event | category | flops | bytes accessed | tf_op | source)
XLA Modules:
  0.0 199.6 jit_solution(13259819882240762609)
XLA Ops:
  6.5 0.0 all-gather.2.cloned.1.call-start
  6.5 0.7 all-gather.2.cloned.1.call-update
  7.3 1.9 copy.37
  9.2 0.1 copy.38
  9.3 25.5 %all_to_all.37 = bf16[128,3,4,512]{0,3,1,2:T(8,128)(2,1)S(1)} all-to-all(bf16[128,3,4,512]{0,3,1,2:T(8,128)(2,1)S(1)} %copy.38), channel_id=1, replica_groups=mesh['seq'=4,'exp'=32] {'seq'}, dimensions={2} | all-to-all | bytes 3145728 | tf_op jit(solution)/shard_map/all_to_all | solution.py:466
  34.7 0.7 copy.39
  35.5 0.1 fusion.15
  35.6 0.2 copy.40
  35.8 0.2 copy.41
  36.0 0.2 copy.44
  36.2 3.5 %fusion.16 = (f32[4,512]{1,0:T(4,128)S(1)}, f32[4,512,512]{1,2,0:T(8,128)}) fusion(bf16[512,4,128]{0,2,1:T(8,128)(2,1)S(1)} %bitcast.39, bf16[512,4,128]{0,2,1:T(8,128)(2,1)S(1)} %bitcast.40), kind=kOutput, calls=%fused_computation.20 | convolution fusion | flops 271581696 | bytes 5251072 | tf_op jit(solution)/shard_map/sub | solution.py:29
  39.7 0.0 copy-start.4
  39.7 0.0 copy-start.3
  39.7 3.1 %fusion.8 = bf16[512,4,128]{2,0,1:T(8,128)(2,1)S(1)} fusion(bf16[512,4,128]{0,2,1:T(8,128)(2,1)S(1)} %bitcast.41, f32[4,512,512]{1,2,0:T(8,128)} %get-tuple-element.9, f32[4,512]{1,0:T(4,128)S(1)} %get-tuple-element.8), kind=kOutput, calls=%fused_computation.12 | convolution fusion | flops 270794752 | bytes 5251072 | tf_op jit(solution)/shard_map/hqk,khd->qhd/dot_general | solution.py:30
  42.8 0.0 copy-start.1
  42.8 0.4 copy.47
  43.2 1.0 all_to_all.31
  44.2 3.7 %all-to-all-start.1 = ((bf16[4,128,512]{2,1,0:T(8,128)(2,1)}), bf16[4,128,512]{2,1,0:T(8,128)(2,1)S(1)}, u32[]{:S(2)}, u32[]{:S(2)}) async-start(bf16[4,128,512]{2,1,0:T(8,128)(2,1)} %all_to_all.31), calls=%async_computation.1 | async-start | bytes 1048576 | tf_op jit(solution)/shard_map/all_to_all | solution.py:473
  47.9 0.0 copy-done.4
  47.9 0.7 copy.49
  48.6 0.0 copy-done.3
  48.6 0.7 copy.50.ids
  49.3 5.7 %all-to-all-done.1 = bf16[4,128,512]{2,1,0:T(8,128)(2,1)S(1)} async-done(((bf16[4,128,512]{2,1,0:T(8,128)(2,1)}), bf16[4,128,512]{2,1,0:T(8,128)(2,1)S(1)}, u32[]{:S(2)}, u32[]{:S(2)}) %all-to-all-start.1) | async-done | bytes 524320 | tf_op jit(solution)/shard_map/all_to_all | solution.py:473
  55.1 0.3 copy.48
  55.3 10.7 %all-gather.2.cloned.1.call-done = bf16[2048,2048]{1,0:T(8,128)(2,1)} async-done(((bf16[64,2048]{1,0:T(8,128)(2,1)}), bf16[2048,2048]{1,0:T(8,128)(2,1)}) %all-gather.2.cloned.1.call-update) | async-done | bytes 8388624 | tf_op jit(solution)/shard_map/all_gather | solution.py:476
  66.1 0.0 copy-done.1
  66.1 0.0 copy-start.2
  66.1 4.7 %fusion.4.mid = bf16[128,2048]{1,0:T(8,128)(2,1)S(1)} fusion(bf16[128,2048]{0,1:T(8,128)(2,1)S(1)} %bitcast.36, bf16[2048,2048]{1,0:T(8,128)(2,1)} %all-gather.2.cloned.1.call-done, bf16[1,128,2048]{2,1,0:T(8,128)(2,1)S(1)} %copy-done.1), kind=kOutput, calls=%fused_computation.6 | convolution fusion | flops 1074528256 | bytes 9961472 | tf_op jit(solution)/shard_map/dot_general | solution.py:474
  70.7 0.0 copy-start
  70.7 0.2 fusion.9
  70.9 0.0 copy-done.2
  70.9 1.0 fusion.11.normed
  71.9 0.0 copy-done
  71.9 118.9 %expert_stage.1 = bf16[128,2048]{1,0:T(8,128)(2,1)} custom-call(bf16[128,2048]{1,0:T(8,128)(2,1)} %fusion.11.normed, bf16[128,2048]{1,0:T(8,128)(2,1)} %copy-done, s32[128,2]{1,0:T(8,128)} %copy.50.ids, s32[2,128]{1,0:T(2,128)} %bitcast.43, f32[128,2]{1,0:T(8,128)} %bitcast.42, bf16[2048,1408]{1,0:T(8,128)(2,1)} %bitcast.33, bf16[2048,1408]{1,0:T(8,128)(2,1)} %bitcast.34, ...), custom_call_target="tpu_custom_call" | custom-call | tf_op jit(solution)/shard_map/expert_stage/pallas_call | solution.py:437
  190.9 1.9 copy.56
  (1 shorter events, 0.0 us)
Async XLA Ops:
  6.5 59.5 %all-gather.2.cloned.1.call-start = ((), (), s32[]{:S(2)}) async-start(), calls=%async_computation.2 | async-start | bytes 8650752 | tf_op jit(solution)/shard_map/all_gather | solution.py:476
  39.7 8.2 %copy-start.4 = (f32[1,128,2]{1,2,0:T(2,128)S(1)}, f32[1,128,2]{1,2,0:T(2,128)}, u32[]{:S(2)}) copy-start(f32[1,128,2]{1,2,0:T(2,128)} %param.14) | copy-start | bytes 3076
  39.7 8.9 %copy-start.3 = (s32[1,128,2]{1,2,0:T(2,128)S(1)}, s32[1,128,2]{1,2,0:T(2,128)}, u32[]{:S(2)}) copy-start(s32[1,128,2]{1,2,0:T(2,128)} %param.13) | copy-start | bytes 3076
  42.8 23.3 %copy-start.1 = (bf16[1,128,2048]{2,1,0:T(8,128)(2,1)S(1)}, bf16[1,128,2048]{2,1,0:T(8,128)(2,1)}, u32[]{:S(2)}) copy-start(bf16[1,128,2048]{2,1,0:T(8,128)(2,1)} %param.10) | copy-start | bytes 1572868
  44.2 10.8 %all-to-all-start.1 = ((bf16[4,128,512]{2,1,0:T(8,128)(2,1)}), bf16[4,128,512]{2,1,0:T(8,128)(2,1)S(1)}, u32[]{:S(2)}, u32[]{:S(2)}) async-start(bf16[4,128,512]{2,1,0:T(8,128)(2,1)} %all_to_all.31), calls=%async_computation.1 | async-start | bytes 1048576 | tf_op jit(solution)/shard_map/all_to_all | solution.py:473
  66.1 4.9 %copy-start.2 = (f32[2048]{0:T(1024)S(1)}, f32[2048]{0:T(1024)}, u32[]{:S(2)}) copy-start(f32[2048]{0:T(1024)} %param.12) | copy-start | bytes 24580
  70.7 1.2 copy-start
Sparse Core Ops, SparseCore 0:
  9.6 56.3 all-gather.1

commit v2 on v1

--- a/solution.py
+++ b/solution.py
@@ -1,5 +1,3 @@
-import functools
-
 import jax
 import jax.numpy as jnp
 from jax import lax
@@ -22,17 +20,6 @@
 QUART = D // 4
 
 
-def attend_block(query_block, key_rows, value_rows):
-    scores = jnp.einsum(
-        "qhd,khd->hqk", query_block, key_rows, preferred_element_type=jnp.float32
-    ) * HEAD_DIM ** (-0.5)
-    attn_probs = jax.nn.softmax(scores, axis=-1).astype(jnp.bfloat16)
-    mixed_heads = jnp.einsum(
-        "hqk,khd->qhd", attn_probs, value_rows, preferred_element_type=jnp.float32
-    )
-    return mixed_heads.astype(jnp.bfloat16)
-
-
 def position():
     s = lax.axis_index("seq")
     e = lax.axis_index("exp")
@@ -94,9 +81,11 @@
     return out
 
 
-def expert_kernel(
-    normed,
-    mid,
+def layer_kernel(
+    qkv_hbm,
+    resid,
+    ow_hbm,
+    gain,
     ids,
     ids_t,
     gates,
@@ -104,6 +93,12 @@
     wu_hbm,
     wd_hbm,
     out,
+    qkv,
+    att,
+    merged,
+    ow,
+    normed,
+    mid,
     wg,
     wu,
     wd,
@@ -124,6 +119,15 @@
     red_f,
     back_m,
     back_f,
+    l_sem,
+    q_s,
+    q_r,
+    h_s,
+    h_r,
+    x_s,
+    x_r,
+    t_s,
+    t_r,
     w_sem,
     ip_s,
     ip_r,
@@ -145,6 +149,7 @@
     up = (lax.rem(s + 1, 4), exp_me)
     down = (lax.rem(s + 3, 4), exp_me)
     zdev = (up, down)
+    across = (lax.rem(s + 2, 4), exp_me)
 
     def remote(src, dst, ss, rs, dev):
         return pltpu.make_async_remote_copy(
@@ -159,7 +164,7 @@
             barrier, inc=1, device_id=plane_device(s, y, x, c, i, 1), device_id_type=MESH
         )
 
-    for dev in zdev:
+    for dev in (up, down, across):
         pl.semaphore_signal(barrier, inc=1, device_id=dev, device_id_type=MESH)
 
     loads = [
@@ -168,6 +173,193 @@
     ]
     for ld in loads:
         ld.start()
+
+    own_cols = pl.multiple_of(s * 512, 512)
+    chip_row = (y * 4 + x) * 128
+    own_ow = pl.ds(pl.multiple_of(chip_row + c * 64, 64), 64)
+    local = [
+        pltpu.make_async_copy(
+            qkv_hbm.at[:, pl.ds(pl.multiple_of(own_cols + p * D, 512), 512)],
+            qkv.at[p, pl.ds(0, TOK)],
+            l_sem.at[p],
+        )
+        for p in range(3)
+    ]
+    local.append(pltpu.make_async_copy(ow_hbm, ow.at[own_ow], l_sem.at[3]))
+    for ld in local:
+        ld.start()
+
+    def seq_peer(r):
+        return (lax.rem(s + r, 4), exp_me)
+
+    def send_head(h, r, p):
+        cols = pl.multiple_of(lax.rem(s + r, 4) * 512 + (p * D + h * HEAD_DIM), HEAD_DIM)
+        return remote(
+            qkv_hbm.at[:, pl.ds(cols, HEAD_DIM)],
+            qkv.at[p, pl.ds((4 - r) * TOK, TOK), pl.ds(h * HEAD_DIM, HEAD_DIM)],
+            q_s.at[h, r - 1, p],
+            q_r.at[h, r - 1, p],
+            seq_peer(r),
+        )
+
+    def return_head(h, r):
+        cols = pl.ds(h * HEAD_DIM, HEAD_DIM)
+        return remote(
+            att.at[r, :, cols],
+            merged.at[4 - r, :, cols],
+            h_s.at[h, r - 1],
+            h_r.at[h, r - 1],
+            seq_peer(r),
+        )
+
+    half_cols = pl.ds(pl.multiple_of(c * 1024, 1024), 1024)
+
+    def chip_at(a, b):
+        ny = lax.rem(y + (1 - c) * b + c * a, 4)
+        nx = lax.rem(x + (1 - c) * a + c * b, 4)
+        return ny * 4 + nx
+
+    def chunk(a, b, part=None):
+        base = chip_at(a, b) * 128
+        size = 128
+        if part is not None:
+            base, size = base + part * 64, 64
+        return ow.at[pl.ds(pl.multiple_of(base, 64), size), half_cols]
+
+    def ring_device(axis, step):
+        other = chip_at(step, 0) if axis == 0 else chip_at(0, step)
+        return (s, other * 2 + c)
+
+    partner = (s, (y * 4 + x) * 2 + 1 - c)
+
+    def ring(axis, a, d):
+        ref = chunk(0, 0) if axis == 0 else chunk(a, 0)
+        at = 4 if axis == 0 else a
+        return remote(
+            ref, ref, x_s.at[at, d, 0], x_r.at[at, d, 0], ring_device(axis, 1 if d == 0 else 3)
+        )
+
+    def ring_relay(axis, a, d):
+        o = 3 if d == 0 else 1
+        ref = chunk(o, 0, d) if axis == 0 else chunk(a, o, d)
+        at = 4 if axis == 0 else a
+        return remote(
+            ref, ref, x_s.at[at, d, 1], x_r.at[at, d, 1], ring_device(axis, 1 if d == 0 else 3)
+        )
+
+    def swap_chip():
+        ref = ow.at[own_ow]
+        return remote(ref, ref, t_s.at[0], t_r.at[0], partner)
+
+    def swap(a, b):
+        ref = chunk(a, b)
+        return remote(ref, ref, t_s.at[a * 4 + b], t_r.at[a * 4 + b], partner)
+
+    pl.semaphore_wait(barrier, 34)
+
+    @pl.loop(0, 4)
+    def _(h):
+        for r in (2, 1, 3):
+            for p in range(3):
+                send_head(h, r, p).start()
+
+    local[3].wait()
+    swap_chip().start()
+    swap_chip().wait_recv()
+    for d in range(2):
+        ring(0, 0, d).start()
+    for d in range(2):
+        ring(1, 0, d).start()
+
+    def first_axis():
+        for d in range(2):
+            ring(0, 0, d).wait_recv()
+            ring_relay(0, 0, d).start()
+        for a in (1, 3):
+            for d in range(2):
+                ring(1, a, d).start()
+        for a in (1, 3):
+            swap(a, 0).start()
+
+    def first_axis_far():
+        for d in range(2):
+            ring_relay(0, 0, d).wait_recv()
+        for d in range(2):
+            ring(1, 2, d).start()
+        swap(2, 0).start()
+
+    def second_axis(a):
+        for d in range(2):
+            ring(1, a, d).wait_recv()
+            ring_relay(1, a, d).start()
+        for b in (1, 3):
+            swap(a, b).start()
+
+    def second_axis_far(a):
+        for d in range(2):
+            ring_relay(1, a, d).wait_recv()
+        swap(a, 2).start()
+
+    scale = HEAD_DIM ** (-0.5) * 1.4426950408889634
+
+    def attend(h):
+        for r in (2, 1, 3):
+            for p in range(3):
+                send_head(h, r, p).wait_recv()
+        cols = slice(h * HEAD_DIM, (h + 1) * HEAD_DIM)
+
+        @pl.loop(0, 4)
+        def _(i):
+            r = lax.rem(i + 1, 4)
+            q = qkv[0, pl.ds(pl.multiple_of(r * TOK, TOK), TOK), cols]
+            scores = lax.dot_general(
+                q, qkv[1, :, cols], (((1,), (1,)), ((), ())), preferred_element_type=F32
+            )
+            top = jnp.max(scores, axis=1, keepdims=True)
+            probs = jnp.exp2((scores - top) * scale)
+            norm = jnp.sum(probs, axis=1, keepdims=True)
+            mixed = jnp.dot(probs.astype(BF), qkv[2, :, cols], preferred_element_type=F32)
+            att[r, :, cols] = (mixed / norm).astype(BF)
+
+        for r in (2, 1, 3):
+            return_head(h, r).start()
+
+    for ld in local[:3]:
+        ld.wait()
+    first_axis()
+    attend(0)
+    second_axis(0)
+    attend(1)
+    first_axis_far()
+    attend(2)
+    second_axis(1)
+    second_axis(3)
+    attend(3)
+    second_axis(2)
+    merged[0] = att[0]
+    for a in (0, 1, 3, 2):
+        second_axis_far(a)
+    for i in range(1, 16):
+        swap(i // 4, i % 4).wait_recv()
+    for h in range(4):
+        for r in (2, 1, 3):
+            return_head(h, r).wait_recv()
+
+    square = jnp.zeros((TOK, 1), F32)
+    for n in range(4):
+        cols = slice(n * 512, (n + 1) * 512)
+        acc = resid[:, cols].astype(F32)
+        for j in range(4):
+            rows_j = pl.ds(pl.multiple_of(lax.rem(s + j, 4) * 512, 512), 512)
+            acc = acc + jnp.dot(merged[j], ow[rows_j, cols], preferred_element_type=F32)
+        rounded = acc.astype(BF)
+        mid[:, cols] = rounded
+        wide = rounded.astype(F32)
+        square = square + jnp.sum(wide * wide, axis=1, keepdims=True)
+    inv = lax.rsqrt(square / D + 1e-06)
+    for n in range(4):
+        cols = slice(n * 512, (n + 1) * 512)
+        normed[:, cols] = (mid[:, cols].astype(F32) * inv * gain[:, cols]).astype(BF)
 
     rows = routes_rows(ids_t[...], y, x, c)
     sub = lax.broadcasted_iota(jnp.int32, (EXPERTS * MAIN, TOK), 0)
@@ -186,8 +378,6 @@
     send_f[...] = fold.astype(BF)
     recv_m[0, 0:MAIN, :] = send_m[0:MAIN, :]
     recv_f[0, 0:MAIN, :] = send_f[0:MAIN, :]
-
-    pl.semaphore_wait(barrier, 33)
 
     def inplane(i):
         dev = plane_device(s, y, x, c, i, 1)
@@ -395,6 +585,20 @@
         for cp in home(lax.div(i, 8), lax.rem(i, 8)):
             cp.wait_send()
 
+    for h in range(4):
+        for r in (2, 1, 3):
+            for p in range(3):
+                send_head(h, r, p).wait_send()
+            return_head(h, r).wait_send()
+    swap_chip().wait_send()
+    for i in range(1, 16):
+        swap(i // 4, i % 4).wait_send()
+    for d in range(2):
+        ring(0, 0, d).wait_send()
+        ring_relay(0, 0, d).wait_send()
+        for a in range(4):
+            ring(1, a, d).wait_send()
+            ring_relay(1, a, d).wait_send()
     for g in range(GROUPS):
         for make in (forward, relay, far, direct, summed):
             for d in range(2):
@@ -402,12 +606,18 @@
                     cp.wait_send()
 
 
-def expert_stage(normed, middle, ids, gates, wg, wu, wd):
+def layer(attn_inputs, residual, out_weight, gain, ids, gates, wg, wu, wd):
     vm = pl.BlockSpec(memory_space=pltpu.VMEM)
     hb = pl.BlockSpec(memory_space=pl.ANY)
     dma = pltpu.SemaphoreType.DMA
     G = GROUPS
     scratch = [
+        pltpu.VMEM((3, 512, 512), BF),
+        pltpu.VMEM((4, TOK, 512), BF),
+        pltpu.VMEM((4, TOK, 512), BF),
+        pltpu.VMEM((D, D), BF),
+        pltpu.VMEM((TOK, D), BF),
+        pltpu.VMEM((TOK, D), BF),
         pltpu.VMEM((D, FFL), BF),
         pltpu.VMEM((D, FFL), BF),
         pltpu.VMEM((FFL, D), BF),
@@ -428,6 +638,15 @@
         pltpu.VMEM((G, 64, QUART), BF),
         pltpu.VMEM((256, D), BF),
         pltpu.VMEM((256, QUART), BF),
+        dma((4,)),
+        dma((4, 3, 3)),
+        dma((4, 3, 3)),
+        dma((4, 3)),
+        dma((4, 3)),
+        dma((5, 2, 2)),
+        dma((5, 2, 2)),
+        dma((16,)),
+        dma((16,)),
         dma((3,)),
         dma((32, 2)),
         dma((32, 2)),
@@ -435,16 +654,16 @@
     scratch += [dma((G, 2, 2)) for _ in range(10)]
     scratch += [dma((32, 2)), dma((32, 2))]
     return pl.pallas_call(
-        expert_kernel,
+        layer_kernel,
         out_shape=jax.ShapeDtypeStruct((TOK, D), BF),
-        in_specs=[vm] * 5 + [hb] * 3,
+        in_specs=[hb, vm, hb] + [vm] * 4 + [hb] * 3,
         out_specs=vm,
         scratch_shapes=scratch,
-        name="expert_stage",
+        name="layer",
         compiler_params=pltpu.CompilerParams(
             collective_id=0, has_side_effects=True, vmem_limit_bytes=60 * 2**20
         ),
-    )(normed, middle, ids, ids.T, gates, wg, wu, wd)
+    )(attn_inputs, residual, out_weight, gain, ids, ids.T, gates, wg, wu, wd)
 
 
 def per_device(
@@ -458,45 +677,18 @@
     up_weight,
     down_weight,
 ):
-    tok_count = attn_inputs.shape[1]
-    seq_count = lax.axis_size("seq")
-    model_width = residual.shape[-1]
-    head_local = HEADS // seq_count
-    laid = attn_inputs.reshape(tok_count, 3, seq_count, head_local * HEAD_DIM)
-    by_heads = lax.all_to_all(laid, "seq", split_axis=2, concat_axis=0, tiled=True)
-    clip_len = by_heads.shape[0]
-    queries = by_heads[:, 0, 0].reshape(clip_len, head_local, HEAD_DIM)
-    keys_all = by_heads[:, 1, 0].reshape(clip_len, head_local, HEAD_DIM)
-    values_all = by_heads[:, 2, 0].reshape(clip_len, head_local, HEAD_DIM)
-    attended = attend_block(queries, keys_all, values_all)
-    attended = attended.reshape(clip_len, head_local * HEAD_DIM)
-    merged = lax.all_to_all(attended, "seq", split_axis=0, concat_axis=1, tiled=True)
-    projected = jnp.dot(
-        merged,
-        lax.all_gather(out_weight, "exp", axis=0, tiled=True),
-        preferred_element_type=jnp.float32,
-    )
-    middle = lax.optimization_barrier(
-        (residual.reshape(tok_count, model_width).astype(jnp.float32) + projected).astype(
-            jnp.bfloat16
-        )
-    )
-    mid_float = middle.astype(jnp.float32)
-    normed = (
-        mid_float
-        * lax.rsqrt(jnp.mean(mid_float * mid_float, axis=-1, keepdims=True) + 1e-06)
-        * norm_gain
-    ).astype(jnp.bfloat16)
-    result = expert_stage(
-        normed,
-        middle,
-        expert_ids.reshape(tok_count, TOP),
-        gate_weights.reshape(tok_count, TOP),
+    result = layer(
+        attn_inputs[0],
+        residual[0],
+        out_weight,
+        norm_gain.reshape(1, D),
+        expert_ids[0],
+        gate_weights[0],
         gate_weight[0],
         up_weight[0],
         down_weight[0],
     )
-    return result.reshape(1, tok_count, model_width)
+    return result.reshape(1, TOK, D)
 
 
 def solution(mesh):

time: 200 us -> 161 us (0.81)
  Pallas kernels: 119 us -> 157 us
  blocking collectives: 25.5 us -> 0 us
  waiting for transfers between devices: 17.1 us -> 0 us
  between operations: 13.5 us -> 0.01 us
  matrix products: 11.2 us -> 0 us
  local copies, waits for them, and re-layouts: 8.48 us -> 4.7 us
  starting transfers between devices: 3.65 us -> 0 us
    pallas_call x1, Pallas kernels: 119 us -> 157 us  [layer(): pl.pallas_call(layer_kernel, out_shape=jax.ShapeDtypeStruct((TOK, D), BF)...]
    all_to_all x1 -> x0, blocking collectives: 25.5 us -> none  [per_device(): lax.all_to_all(laid, 'seq', split_axis=2, concat_axis=0, tiled=True)]
    all_gather x1 -> x0, waiting for transfers between devices: 10.7 us -> none  [per_device(): lax.all_gather(out_weight, 'exp', axis=0, tiled=True)]
    dot_general x2 -> x0, matrix products: 7.79 us -> none  [the longest x1 4.67 us: per_device(): jnp.dot(merged, lax.all_gather(out_weight, 'exp', axis=0, tiled=True), pr...]
    all_to_all x1 -> x0, waiting for transfers between devices: 5.71 us -> none  [per_device(): lax.all_to_all(attended, 'seq', split_axis=0, concat_axis=1, tiled=True)]
    all_to_all x1 -> x0, starting transfers between devices: 3.65 us -> none  [per_device(): lax.all_to_all(attended, 'seq', split_axis=0, concat_axis=1, tiled=True)]
    sub x1 -> x0, matrix products: 3.45 us -> none  [attend_block(): attn_probs = jax.nn.softmax(scores, axis=-1).astype(jnp.bfloat16)]
    unnamed x13 -> x2, local copies, waits for them, and re-layouts: 4.54 us -> 3.29 us
  transfers between devices with their start and end apart: 2 -> 0, of which waited for: 2 -> 0; matrix products, arithmetic and copies ran while one was open for 6% -> 0% of each run, Pallas kernels for 0% -> 0%
where the time goes in v2:
time: 161 us
  Pallas kernels  157 us (98%)
  local copies, waits for them, and re-layouts  4.7 us (3%)
    pallas_call x1, Pallas kernels, layer(): pl.pallas_call(layer_kernel, out_shape=jax.ShapeDtypeStruct((TOK, D), BF)...  157 us
    unnamed x2, local copies, waits for them, and re-layouts  3.29 us

profile of v2, /device:TPU:1, one launch (start us, length us, event | category | flops | bytes accessed | tf_op | source)
XLA Modules:
  0.0 161.3 jit_solution(2632301152975222787)
XLA Ops:
  0.0 1.4 copy.10
  1.4 1.4 copy.11.ids
  2.8 156.6 %layer.1 = bf16[128,2048]{1,0:T(8,128)(2,1)} custom-call(bf16[128,6144]{1,0:T(8,128)(2,1)} %bitcast.15, bf16[128,2048]{1,0:T(8,128)(2,1)} %bitcast.16, bf16[64,2048]{1,0:T(8,128)(2,1)} %ow_hbm.1, f32[1,2048]{1,0:T(1,128)} %bitcast.18, s32[128,2]{1,0:T(8,128)} %copy.11.ids, s32[2,128]{1,0:T(2,128)} %bitcast.20, f32[128,2]{1,0:T(8,128)} %bitcast.17, ...), custom_call_target="tpu_custom_call" | custom-call | tf_op jit(solution)/shard_map/layer/pallas_call | solution.py:656
  159.4 1.9 %copy.13 = bf16[1,128,2048]{2,1,0:T(8,128)(2,1)} copy(bf16[1,128,2048]{2,1,0:T(8,128)(2,1)} %bitcast.14) | data formatting | bytes 1048576
